TPU v7x, 256 devices: a whole 4x4x8 slice. The times are simulated.
256 devices in a mesh: blk: 64 (over x, z, y_hi), col: 4 (over y_lo, core).
Axes of the slice: x: 4, y: 4 (y_hi: 2, y_lo: 2; y = y_hi * 2 + y_lo), z: 8, core: 2. Of those that a mesh axis runs over, the one named last changes fastest.
Arguments:
- points: bfloat16 [32768, 128], P(('blk', 'col')), may hold values from -4.5 to 4.5
- targets: float32 [32768, 32], P(('blk', 'col')), may hold values from -6 to 6
- pivots: int32 [2, 256], replicated, may hold values from 0 to 32767, as said below
Outputs:
- factor: bfloat16 [32768, 512], P(('blk', 'col'))
- solution: float32 [32768, 32], P(('blk', 'col'))
- residual: float32 [32768, 32], P(('blk', 'col'))
Inputs may be any that keep to these rules, and one draw needn't show every extreme that they name: `pivots`: the 512 indices are distinct; 0 and 32767 are among them.
All inputs are finite; a program needn't handle non-finite values.
Results may differ from a plain program's by a relative error of at most 0.012.
Values may be sent and summed in bfloat16 or wider, within the bound.
No kernel may reach another device: no remote copies, remote signals or barrier semaphores. Data moves between devices by JAX's collectives and lax.ppermute only.
A program may use at most 64 MiB of HBM per device.

v0:
```python
import jax
import jax.numpy as jnp
from jax import lax
from jax.sharding import PartitionSpec as P

FEATURES = 128
ITERS = 3
noise_level = 0.5
jitter_level = 0.05
highest = lax.Precision.HIGHEST


def squared_norms(point_rows):
    wide_rows = point_rows.astype(jnp.float32)
    return jnp.sum(wide_rows * wide_rows, axis=1)


def kernel_block(left_rows, left_norms, right_rows, right_norms):
    inner = lax.dot_general(
        left_rows, right_rows, (((1,), (1,)), ((), ())), preferred_element_type=jnp.float32
    )
    distance = left_norms[:, None] + right_norms[None, :] - 2.0 * inner
    return jnp.exp(-2.0 * distance / FEATURES)


def lower_solve(lower_factor, right_rows):
    return jax.scipy.linalg.solve_triangular(lower_factor, right_rows.T, lower=True).T


def build_factor(point_rows, first_pick, second_pick):
    row_norms = squared_norms(point_rows)
    first_norms = squared_norms(first_pick)
    second_norms = squared_norms(second_pick)
    identity_piv = jnp.eye(first_pick.shape[0], dtype=jnp.float32)
    first_chol = jnp.linalg.cholesky(
        kernel_block(first_pick, first_norms, first_pick, first_norms) + jitter_level * identity_piv
    )
    first_coef = lower_solve(
        first_chol, kernel_block(point_rows, row_norms, first_pick, first_norms)
    )
    shared_coef = lower_solve(
        first_chol, kernel_block(second_pick, second_norms, first_pick, first_norms)
    )
    schur_block = (
        kernel_block(second_pick, second_norms, second_pick, second_norms)
        + jitter_level * identity_piv
        - jnp.dot(shared_coef, shared_coef.T, precision=highest)
    )
    second_chol = jnp.linalg.cholesky(schur_block)
    second_cross = kernel_block(point_rows, row_norms, second_pick, second_norms) - jnp.dot(
        first_coef, shared_coef.T, precision=highest
    )
    second_coef = lower_solve(second_chol, second_cross)
    return jnp.concatenate([first_coef, second_coef], axis=1)


def per_device(points, targets, pivots):
    row_count = points.shape[0]
    piv_count = pivots.shape[1]
    shard_index = lax.axis_index("blk") * lax.axis_size("col") + lax.axis_index("col")
    first_row = shard_index * row_count
    flat_pivots = pivots.reshape(-1)
    owned = (
        flat_pivots[:, None] == first_row + jnp.arange(row_count, dtype=jnp.int32)[None, :]
    ).astype(jnp.float32)
    local_pick = jnp.dot(owned, points.astype(jnp.float32), precision=highest)
    picked = lax.psum(local_pick, ("blk", "col")).astype(jnp.bfloat16)
    wide_factor = build_factor(points, picked[:piv_count], picked[piv_count:])
    factor = wide_factor.astype(jnp.bfloat16)
    local_gram = lax.dot_general(
        wide_factor, wide_factor, (((0,), (0,)), ((), ())), precision=highest
    )
    gram = lax.psum(local_gram, ("blk", "col"))
    gram = gram + noise_level * jnp.eye(2 * piv_count, dtype=jnp.float32)
    gram_chol = jnp.linalg.cholesky(gram)

    def precondition(residual_now):
        local_proj = lax.dot_general(
            wide_factor, residual_now, (((0,), (0,)), ((), ())), precision=highest
        )
        projection = lax.psum(local_proj, ("blk", "col"))
        coefficients = jax.scipy.linalg.cho_solve((gram_chol, True), projection)
        scaled = (
            residual_now - jnp.dot(wide_factor, coefficients, precision=highest)
        ) / noise_level
        return (scaled, lax.psum(jnp.sum(residual_now * scaled, axis=0), ("blk", "col")))

    own_block = lax.all_gather(points, "col", axis=0, tiled=True)
    own_norms = squared_norms(own_block)

    def tile_add(total, key_rows, key_norms, direction_rows):
        weights = kernel_block(own_block, own_norms, key_rows, key_norms)
        return total + jnp.dot(weights, direction_rows, precision=highest)

    solution = jnp.zeros_like(targets)
    residual = targets
    direction_now, inner_now = precondition(residual)
    for step_index in range(ITERS):
        empty = jnp.zeros((own_block.shape[0], direction_now.shape[1]), jnp.float32)
        add_key_rows = lax.all_gather(points.astype(jnp.float32), "blk", axis=0, tiled=True).astype(
            jnp.bfloat16
        )
        fold_direction_rows = lax.all_gather(direction_now, "blk", axis=0, tiled=True)
        piece_rows = add_key_rows.shape[0]
        splits = piece_rows // row_count

        def scan_step(carry, operands):
            return (tile_add(carry, operands[0], operands[1], operands[2]), None)

        stacked = (
            add_key_rows.reshape(splits, row_count, add_key_rows.shape[1]),
            squared_norms(add_key_rows).reshape(splits, row_count),
            fold_direction_rows.reshape(splits, row_count, fold_direction_rows.shape[1]),
        )
        result, unused = lax.scan(scan_step, empty, stacked)
        image = (
            lax.psum_scatter(result, "col", scatter_dimension=0, tiled=True)
            + noise_level * direction_now
        )
        curvature = lax.psum(jnp.sum(direction_now * image, axis=0), ("blk", "col"))
        step_size = inner_now / curvature
        solution = solution + step_size * direction_now
        residual = residual - step_size * image
        if step_index + 1 < ITERS:
            scaled, inner_next = precondition(residual)
            direction_now = scaled + inner_next / inner_now * direction_now
            inner_now = inner_next
    return (factor, solution, residual)


def solution(mesh):
    return jax.shard_map(
        per_device,
        mesh=mesh,
        in_specs=(P(("blk", "col"), None), P(("blk", "col"), None), P()),
        out_specs=(P(("blk", "col"), None), P(("blk", "col"), None), P(("blk", "col"), None)),
        check_vma=False,
    )
```

profile of v0, /device:TPU:1, one launch (start us, length us, event | category | flops | bytes accessed | tf_op | source)
XLA Modules:
  0.0 2410.5 jit_solution(17141482593332180947)
XLA Ops:
  8.9 82.6 %all-reduce.14 = bf16[512,128]{1,0:T(8,128)(2,1)S(1)} all-reduce(f32[512,128]{1,0:T(8,128)S(1)} %fusion.57), channel_id=1, replica_groups=mesh['blk'=64,'col'=4] {'blk','col'}, use_global_device_ids=true, to_apply=%region_0.0 | all-reduce | flops 65536 | bytes 393216 | tf_op jit(solution)/shard_map/psum | solution.py:67
  92.1 11.7 cholesky.354
  103.9 9.8 custom-call.54
  114.3 11.7 cholesky.364
  129.2 4.4 while.53
  130.0 1.4 dynamic-slice.27
  132.1 1.4 dynamic-slice.27
  133.6 19.7 custom-call.55
  156.1 11.7 cholesky.381
  167.8 9.8 custom-call.56
  178.1 11.7 cholesky.391
  192.9 4.0 while.54
  193.5 1.4 bitcast_dynamic-update-slice_fusion.7
  195.5 1.4 bitcast_dynamic-update-slice_fusion.7
  196.9 19.7 custom-call.57
  218.0 2.0 fusion.240
  221.1 251.4 %all-reduce.13.cloned.1.call-done = (f32[512,512]{1,0:T(8,128)}, f32[512,32]{0,1:T(8,128)}) async-done(((f32[512,512]{1,0:T(8,128)}, f32[512,32]{0,1:T(8,128)}), (f32[512,512]{1,0:T(8,128)}, f32[512,32]{0,1:T(8,128)})) %all-reduce.13.cloned.1.call-update) | async-done | bytes 1114128 | tf_op jit(solution)/shard_map/psum | solution.py:73
  472.5 1.4 select_add_fusion
  474.5 11.7 cholesky.166
  486.4 9.8 custom-call.42
  496.9 11.7 cholesky.189
  509.9 10.0 custom-call.43
  520.5 11.7 cholesky.292
  533.0 9.8 custom-call.58
  543.4 11.7 cholesky.305
  558.7 10.4 while.55
  559.3 2.0 bitcast_dynamic-update-slice_fusion.8
  561.9 2.0 bitcast_dynamic-update-slice_fusion.8
  564.5 2.0 bitcast_dynamic-update-slice_fusion.8
  567.1 2.0 bitcast_dynamic-update-slice_fusion.8
  569.1 40.1 %custom-call.59 = f32[4,128,128]{1,2,0:T(8,128)S(1)} custom-call(f32[4,128,128]{2,1,0:T(8,128)} %get-tuple-element.393), custom_call_target="InvertDiagBlocksLowerTriangular" | custom-call | tf_op jit(solution)/shard_map/jit(_cho_solve)/triangular_solve | solution.py:82
  614.2 6.7 all_gather.17
  621.0 92.2 %all-gather.7.cloned.1.call-done = f32[8192,32]{0,1:T(8,128)} async-done(((f32[128,32]{0,1:T(8,128)}), f32[8192,32]{0,1:T(8,128)}) %all-gather.7.cloned.1.call-update) | async-done | bytes 1048592 | tf_op jit(solution)/shard_map/all_gather | solution.py:103
  713.2 3.6 copy.29
  716.7 116.0 %all-gather.5.cloned.1.call-done = bf16[8192,128]{1,0:T(8,128)(2,1)} async-done(((bf16[128,128]{1,0:T(8,128)(2,1)}), bf16[8192,128]{1,0:T(8,128)(2,1)}) %all-gather.5.cloned.1.call-update) | async-done | bytes 2097168 | tf_op jit(solution)/shard_map/all_gather | solution.py:100
  832.7 2.7 multiply_reduce_fusion
  835.5 144.7 %while.50 = (s32[]{:T(128)}, f32[512,32]{0,1:T(8,128)S(1)}, f32[512]{0:T(512)S(1)}, f32[64,128]{1,0:T(8,128)S(1)}, bf16[64,128,128]{2,1,0:T(8,128)(2,1)}, /*inde...) while((s32[]{:T(128)}, f32[512,32]{0,1:T(8,128)S(1)}, ...), condition=%wide.region_23.28_spmd.clone, body=%wide.region_22.27_spmd.clone.sunk | while | flops 42237952 | bytes 889451 | solution.py:115
  980.9 20.1 reduce-scatter.4.cloned.1.call-done
  1001.8 77.0 %all-reduce.2 = (f32[32]{0:T(128)S(1)}, f32[32]{0:T(128)S(1)}) all-reduce(f32[32]{0:T(128)S(1)} %get-tuple-element.431, f32[32]{0:T(128)S(1)} %get-tuple-element.430), channel_id=1, replica_groups=mesh['blk'=64,'col'=4] {'blk','col'}, use_global_device_ids=true, to_apply=%region_19.24 | all-reduce | flops 64 | bytes 512 | tf_op jit(solution)/shard_map/psum | solution.py:86
  1079.9 234.4 %all-reduce.9.cloned.1.call-done = f32[512,32]{0,1:T(8,128)} async-done(((f32[512,32]{0,1:T(8,128)}), f32[512,32]{0,1:T(8,128)}) %all-reduce.9.cloned.1.call-update) | async-done | bytes 65552 | tf_op jit(solution)/shard_map/psum | solution.py:81
  1320.8 74.4 %psum.83 = f32[32]{0:T(128)S(1)} all-reduce(f32[32]{0:T(128)S(1)} %get-tuple-element.537), channel_id=1, replica_groups=mesh['blk'=64,'col'=4] {'blk','col'}, use_global_device_ids=true, to_apply=%region_29.34 | all-reduce | flops 32 | bytes 256 | tf_op jit(solution)/shard_map/psum | solution.py:86
  1396.0 95.6 %all-gather.9.cloned.1.call-done = f32[8192,32]{0,1:T(8,128)} async-done(((f32[128,32]{0,1:T(8,128)}), f32[8192,32]{0,1:T(8,128)}) %all-gather.9.cloned.1.call-update) | async-done | bytes 1048592 | tf_op jit(solution)/shard_map/all_gather | solution.py:103
  1491.5 3.6 copy.30
  1495.1 144.7 %while.51 = (s32[]{:T(128)}, f32[512,32]{0,1:T(8,128)S(1)}, f32[512]{0:T(512)S(1)}, f32[64,128]{1,0:T(8,128)S(1)}, bf16[64,128,128]{2,1,0:T(8,128)(2,1)}, /*inde...) while((s32[]{:T(128)}, f32[512,32]{0,1:T(8,128)S(1)}, ...), condition=%wide.region_31.36_spmd.clone, body=%wide.region_30.35_spmd.clone.sunk | while | flops 42237952 | bytes 889451 | solution.py:115
  1507.4 1.2 convolution_add_fusion.7
  1511.9 1.2 convolution_add_fusion.7
  1516.5 1.2 convolution_add_fusion.7
  1525.5 1.2 convolution_add_fusion.7
  1530.0 1.2 convolution_add_fusion.7
  1543.6 1.2 convolution_add_fusion.7
  1548.1 1.2 convolution_add_fusion.7
  1561.7 1.2 convolution_add_fusion.7
  1566.2 1.2 convolution_add_fusion.7
  1575.2 1.2 convolution_add_fusion.7
  1640.5 21.1 reduce-scatter.6.cloned.1.call-done
  1662.4 77.3 %psum.84 = f32[32]{0:T(128)S(1)} all-reduce(f32[32]{0:T(128)S(1)} %multiply_reduce_fusion.7), channel_id=1, replica_groups=mesh['blk'=64,'col'=4] {'blk','col'}, use_global_device_ids=true, to_apply=%region_34.39 | all-reduce | flops 32 | bytes 256 | tf_op jit(solution)/shard_map/psum | solution.py:120
  1741.6 234.4 %all-reduce.11.cloned.1.call-done = f32[512,32]{0,1:T(8,128)} async-done(((f32[512,32]{0,1:T(8,128)}), f32[512,32]{0,1:T(8,128)}) %all-reduce.11.cloned.1.call-update) | async-done | bytes 65552 | tf_op jit(solution)/shard_map/psum | solution.py:81
  1982.4 74.4 %psum.86 = f32[32]{0:T(128)S(1)} all-reduce(f32[32]{0:T(128)S(1)} %get-tuple-element.539), channel_id=1, replica_groups=mesh['blk'=64,'col'=4] {'blk','col'}, use_global_device_ids=true, to_apply=%region_37.42 | all-reduce | flops 32 | bytes 256 | tf_op jit(solution)/shard_map/psum | solution.py:86
  2057.6 95.6 %all-gather.11.cloned.1.call-done = f32[8192,32]{0,1:T(8,128)} async-done(((f32[128,32]{0,1:T(8,128)}), f32[8192,32]{0,1:T(8,128)}) %all-gather.11.cloned.1.call-update) | async-done | bytes 1048592 | tf_op jit(solution)/shard_map/all_gather | solution.py:103
  2153.2 3.6 copy.31
  2156.8 144.7 %while.52 = (s32[]{:T(128)}, f32[512,32]{0,1:T(8,128)S(1)}, f32[512]{0:T(512)S(1)}, f32[64,128]{1,0:T(8,128)S(1)}, bf16[64,128,128]{2,1,0:T(8,128)(2,1)}, /*inde...) while((s32[]{:T(128)}, f32[512,32]{0,1:T(8,128)S(1)}, ...), condition=%wide.region_39.44_spmd.clone, body=%wide.region_38.43_spmd.clone.sunk | while | flops 42237952 | bytes 889451 | solution.py:115
  2302.1 21.1 reduce-scatter.8.cloned.1.call-done
  2324.8 77.0 %psum.87 = f32[32]{0:T(128)S(1)} all-reduce(f32[32]{0:T(128)S(1)} %multiply_reduce_fusion.5), channel_id=1, replica_groups=mesh['blk'=64,'col'=4] {'blk','col'}, use_global_device_ids=true, to_apply=%region_42.47 | all-reduce | flops 32 | bytes 256 | tf_op jit(solution)/shard_map/psum | solution.py:120
  2401.8 1.4 multiply_subtract_fusion
  (767 shorter events, 463.6 us)
Async XLA Ops:
  7.2 119.0 %copy-start.5 = (bf16[128,128]{1,0:T(8,128)(2,1)S(1)}, bf16[128,128]{1,0:T(8,128)(2,1)}, u32[]{:S(2)}) copy-start(bf16[128,128]{1,0:T(8,128)(2,1)} %param.16) | copy-start | bytes 98308
  7.2 465.3 %all-reduce.13.cloned.1.call-start = ((), (), s32[]{:S(2)}) async-start(), calls=%async_computation.12 | async-start | bytes 2228224 | tf_op jit(solution)/shard_map/psum | solution.py:73
  154.5 65.5 %copy-start.8 = (f32[128,32]{0,1:T(8,128)S(1)}, f32[128,32]{0,1:T(8,128)}, u32[]{:S(2)}) copy-start(f32[128,32]{0,1:T(8,128)} %param.17) | copy-start | bytes 49156
  221.1 492.1 %all-gather.7.cloned.1.call-start = ((), (), s32[]{:S(2)}) async-start(), calls=%async_computation.4 | async-start | bytes 1064960 | tf_op jit(solution)/shard_map/all_gather | solution.py:103
  472.5 1.8 copy-start
  474.5 134.7 %copy-start.9 = (f32[512,32]{0,1:T(8,128)S(1)}, f32[512,32]{0,1:T(8,128)}, u32[]{:S(2)}) copy-start(f32[512,32]{0,1:T(8,128)} %get-tuple-element.501) | copy-start | bytes 196612
  496.5 117.6 %copy-start.6 = (bf16[128,128]{1,0:T(8,128)(2,1)S(1)}, bf16[128,128]{1,0:T(8,128)(2,1)}, u32[]{:S(2)}) copy-start(bf16[128,128]{1,0:T(8,128)(2,1)} %param.16) | copy-start | bytes 98308
  613.3 219.4 %all-gather.5.cloned.1.call-start = ((), (), s32[]{:S(2)}) async-start(), calls=%async_computation.3 | async-start | bytes 2129920 | tf_op jit(solution)/shard_map/all_gather | solution.py:100
  614.1 386.8 %reduce-scatter.4.cloned.1.call-start = ((), (), s32[]{:S(2)}) async-start(), calls=%async_computation.5 | async-start | bytes 81920 | tf_op jit(solution)/shard_map/reduce_scatter | solution.py:117
  980.2 0.6 copy-start.1
  980.8 333.5 %all-reduce.9.cloned.1.call-start = ((), (), s32[]{:S(2)}) async-start(), calls=%async_computation.6 | async-start | bytes 131072 | tf_op jit(solution)/shard_map/psum | solution.py:81
  1079.9 411.7 %all-gather.9.cloned.1.call-start = ((), (), s32[]{:S(2)}) async-start(), calls=%async_computation.7 | async-start | bytes 1064960 | tf_op jit(solution)/shard_map/all_gather | solution.py:103
  1395.9 265.7 %reduce-scatter.6.cloned.1.call-start = ((), (), s32[]{:S(2)}) async-start(), calls=%async_computation.8 | async-start | bytes 81920 | tf_op jit(solution)/shard_map/reduce_scatter | solution.py:117
  1396.0 265.6 %copy-start.4 = (f32[128,32]{0,1:T(8,128)S(1)}, f32[128,32]{0,1:T(8,128)}, u32[]{:S(2)}) copy-start(f32[128,32]{0,1:T(8,128)} %multiply_add_fusion.4) | copy-start | bytes 49156
  1639.8 0.6 copy-start.2
  1640.5 335.5 %all-reduce.11.cloned.1.call-start = ((), (), s32[]{:S(2)}) async-start(), calls=%async_computation.9 | async-start | bytes 131072 | tf_op jit(solution)/shard_map/psum | solution.py:81
  1741.5 411.7 %all-gather.11.cloned.1.call-start = ((), (), s32[]{:S(2)}) async-start(), calls=%async_computation.10 | async-start | bytes 1064960 | tf_op jit(solution)/shard_map/all_gather | solution.py:103
  2057.5 265.7 %reduce-scatter.8.cloned.1.call-start = ((), (), s32[]{:S(2)}) async-start(), calls=%async_computation.11 | async-start | bytes 81920 | tf_op jit(solution)/shard_map/reduce_scatter | solution.py:117
  2057.6 265.6 %copy-start.7 = (f32[128,32]{0,1:T(8,128)S(1)}, f32[128,32]{0,1:T(8,128)}, u32[]{:S(2)}) copy-start(f32[128,32]{0,1:T(8,128)} %multiply_add_fusion.2) | copy-start | bytes 49156
  2301.4 0.6 copy-start.3
Sparse Core Ops, SparseCore 0:
  221.2 251.2 all-reduce.12
  613.5 99.6 all-gather.6
  717.3 115.3 all-gather.4
  981.0 19.9 reduce-scatter.3
  1080.0 234.2 all-reduce.8
  1396.0 95.4 all-gather.8
  1640.6 20.9 reduce-scatter.5
  1741.6 234.2 all-reduce.10
  2057.6 95.4 all-gather.10
  2302.2 20.9 reduce-scatter.7
where the time goes:
time: 2440 us; the launch traced here: 2410 us
  waiting for transfers between devices  1180 us (48%)
  blocking collectives  469 us (19%)
  matrix products  455 us (19%)
  other arithmetic  239 us (10%)
  local copies, waits for them, and re-layouts  35.5 us (1%)
    psum x2, waiting for transfers between devices, precondition(): projection = lax.psum(local_proj, ('blk', 'col'))  469 us
    all_gather x3, waiting for transfers between devices, per_device(): lax.all_gather(direction_now, 'blk', axis=0, tiled=True)  283 us
    psum x1, waiting for transfers between devices, per_device(): gram = lax.psum(local_gram, ('blk', 'col'))  251 us
    dot_general x192, matrix products, tile_add(): return total + jnp.dot(weights, direction_rows, precision=highest)  238 us
    psum x3, blocking collectives, precondition(): lax.psum(jnp.sum(residual_now * scaled, axis=0), ('blk', 'col'))  226 us
    dot_general x197, matrix products, kernel_block(): lax.dot_general(left_rows, right_rows, (((1,), (1,)), ((), ())), preferre...  187 us
    psum x2, blocking collectives, per_device(): curvature = lax.psum(jnp.sum(direction_now * image, axis=0), ('blk', 'col'))  154 us
    all_gather x1, waiting for transfers between devices, per_device(): lax.all_gather(points.astype(jnp.float32), 'blk', axis=0, tiled=True)  116 us
  transfers between devices with their start and end apart: 10, of which 10 were waited for; matrix products, arithmetic and copies ran while one was open for 0% of the time, Pallas kernels for 0%

commit v1 on v0

--- a/solution.py
+++ b/solution.py
@@ -70,7 +70,8 @@
     local_gram = lax.dot_general(
         wide_factor, wide_factor, (((0,), (0,)), ((), ())), precision=highest
     )
-    gram = lax.psum(local_gram, ("blk", "col"))
+    partial = lax.psum(local_gram, "blk")
+    gram = lax.psum(partial, "col")
     gram = gram + noise_level * jnp.eye(2 * piv_count, dtype=jnp.float32)
     gram_chol = jnp.linalg.cholesky(gram)
 

time: 2440 us -> 3030 us (1.24)
  waiting for transfers between devices: 1180 us -> 1770 us
    psum x1 -> x2, waiting for transfers between devices: 251 us -> 734 us  [the longest x1 645 us: per_device(): partial = lax.psum(local_gram, 'blk')]
    psum x2 -> x3, waiting for transfers between devices: 469 us -> 577 us  [precondition(): projection = lax.psum(local_proj, ('blk', 'col'))]
  transfers between devices with their start and end apart: 10 -> 12, of which waited for: 10 -> 12; matrix products, arithmetic and copies ran while one was open for 0% -> 5% of each run, Pallas kernels for 0% -> 0%
where the time goes in v1:
time: 3030 us; the launch traced here: 3000 us
  waiting for transfers between devices  1770 us (58%)
  blocking collectives  468 us (15%)
  matrix products  457 us (15%)
  other arithmetic  239 us (8%)
  local copies, waits for them, and re-layouts  35.8 us (1%)
    psum x1, waiting for transfers between devices, per_device(): partial = lax.psum(local_gram, 'blk')  645 us
    psum x3, waiting for transfers between devices, precondition(): projection = lax.psum(local_proj, ('blk', 'col'))  577 us
    all_gather x3, waiting for transfers between devices, per_device(): lax.all_gather(direction_now, 'blk', axis=0, tiled=True)  294 us
    dot_general x192, matrix products, tile_add(): return total + jnp.dot(weights, direction_rows, precision=highest)  238 us
    psum x3, blocking collectives, precondition(): lax.psum(jnp.sum(residual_now * scaled, axis=0), ('blk', 'col'))  226 us
    dot_general x197, matrix products, kernel_block(): lax.dot_general(left_rows, right_rows, (((1,), (1,)), ((), ())), preferre...  187 us
    psum x2, blocking collectives, per_device(): curvature = lax.psum(jnp.sum(direction_now * image, axis=0), ('blk', 'col'))  154 us
    all_gather x1, waiting for transfers between devices, per_device(): lax.all_gather(points.astype(jnp.float32), 'blk', axis=0, tiled=True)  101 us
  transfers between devices with their start and end apart: 12, of which 12 were waited for; matrix products, arithmetic and copies ran while one was open for 5% of the time, Pallas kernels for 0%

profile of v1, /device:TPU:1, one launch (start us, length us, event | category | flops | bytes accessed | tf_op | source)
XLA Modules:
  0.0 3000.5 jit_solution(11560901591662236084)
XLA Ops:
  8.9 82.6 %all-reduce.19 = bf16[512,128]{1,0:T(8,128)(2,1)S(1)} all-reduce(f32[512,128]{1,0:T(8,128)S(1)} %fusion.57), channel_id=1, replica_groups=mesh['blk'=64,'col'=4] {'blk','col'}, use_global_device_ids=true, to_apply=%region_0.0 | all-reduce | flops 65536 | bytes 393216 | tf_op jit(solution)/shard_map/psum | solution.py:67
  92.1 11.7 cholesky.354
  103.9 9.8 custom-call.54
  114.3 11.7 cholesky.364
  129.2 4.4 while.53
  130.0 1.4 dynamic-slice.27
  132.1 1.4 dynamic-slice.27
  133.6 19.7 custom-call.55
  156.1 11.7 cholesky.381
  167.8 9.8 custom-call.56
  178.1 11.7 cholesky.391
  192.9 4.0 while.54
  193.5 1.4 bitcast_dynamic-update-slice_fusion.7
  195.5 1.4 bitcast_dynamic-update-slice_fusion.7
  196.9 19.7 custom-call.57
  218.0 2.0 fusion.240
  220.1 644.6 %all-reduce.10.cloned.1.call-done = f32[512,512]{1,0:T(8,128)} async-done(((f32[512,512]{1,0:T(8,128)}), f32[512,512]{1,0:T(8,128)}) %all-reduce.10.cloned.1.call-update) | async-done | bytes 1048592 | tf_op jit(solution)/shard_map/psum | solution.py:73
  866.5 89.6 %all-reduce.12.cloned.1.call-done = f32[512,512]{1,0:T(8,128)} async-done(((f32[512,512]{1,0:T(8,128)}), f32[512,512]{1,0:T(8,128)}) %all-reduce.12.cloned.1.call-update) | async-done | bytes 1048592 | tf_op jit(solution)/shard_map/psum | solution.py:74
  956.1 1.4 select_add_fusion
  958.1 11.7 cholesky.166
  970.0 9.8 custom-call.42
  980.5 11.7 cholesky.189
  993.6 9.9 custom-call.43
  1004.2 11.7 cholesky.292
  1016.6 9.8 custom-call.58
  1027.0 11.7 cholesky.305
  1042.3 10.8 while.55
  1043.0 2.0 bitcast_dynamic-update-slice_fusion.8
  1045.7 2.0 bitcast_dynamic-update-slice_fusion.8
  1048.4 2.0 bitcast_dynamic-update-slice_fusion.8
  1051.1 2.0 bitcast_dynamic-update-slice_fusion.8
  1053.1 40.1 %custom-call.59 = f32[4,128,128]{1,2,0:T(8,128)S(1)} custom-call(f32[4,128,128]{2,1,0:T(8,128)} %get-tuple-element.393), custom_call_target="InvertDiagBlocksLowerTriangular" | custom-call | tf_op jit(solution)/shard_map/jit(_cho_solve)/triangular_solve | solution.py:83
  1093.2 108.8 %all-reduce.14.cloned.1.call-done = f32[512,32]{0,1:T(8,128)} async-done(((f32[512,32]{0,1:T(8,128)}), f32[512,32]{0,1:T(8,128)}) %all-reduce.14.cloned.1.call-update) | async-done | bytes 65552 | tf_op jit(solution)/shard_map/psum | solution.py:82
  1209.1 5.2 all_gather.17
  1214.4 101.4 %all-gather.5.cloned.1.call-done = bf16[8192,128]{1,0:T(8,128)(2,1)} async-done(((bf16[128,128]{1,0:T(8,128)(2,1)}), bf16[8192,128]{1,0:T(8,128)(2,1)}) %all-gather.5.cloned.1.call-update) | async-done | bytes 2097168 | tf_op jit(solution)/shard_map/all_gather | solution.py:101
  1315.8 2.7 multiply_reduce_fusion
  1318.5 102.4 %all-gather.7.cloned.1.call-done = f32[8192,32]{0,1:T(8,128)} async-done(((f32[128,32]{0,1:T(8,128)}), f32[8192,32]{0,1:T(8,128)}) %all-gather.7.cloned.1.call-update) | async-done | bytes 1048592 | tf_op jit(solution)/shard_map/all_gather | solution.py:104
  1421.0 3.6 copy.29
  1424.5 144.7 %while.50 = (s32[]{:T(128)}, f32[512,32]{0,1:T(8,128)S(1)}, f32[512]{0:T(512)S(1)}, f32[64,128]{1,0:T(8,128)S(1)}, bf16[64,128,128]{2,1,0:T(8,128)(2,1)}, /*inde...) while((s32[]{:T(128)}, f32[512,32]{0,1:T(8,128)S(1)}, ...), condition=%wide.region_24.29_spmd.clone, body=%wide.region_23.28_spmd.clone.sunk | while | flops 42237952 | bytes 889451 | solution.py:116
  1430.0 1.2 convolution_add_fusion.6
  1439.1 1.2 convolution_add_fusion.6
  1443.6 1.2 convolution_add_fusion.6
  1448.1 1.2 convolution_add_fusion.6
  1457.2 1.2 convolution_add_fusion.6
  1461.7 1.2 convolution_add_fusion.6
  1475.3 1.2 convolution_add_fusion.6
  1479.8 1.2 convolution_add_fusion.6
  1569.9 21.1 reduce-scatter.4.cloned.1.call-done
  1591.8 77.0 %all-reduce.2 = (f32[32]{0:T(128)S(1)}, f32[32]{0:T(128)S(1)}) all-reduce(f32[32]{0:T(128)S(1)} %get-tuple-element.431, f32[32]{0:T(128)S(1)} %get-tuple-element.430), channel_id=1, replica_groups=mesh['blk'=64,'col'=4] {'blk','col'}, use_global_device_ids=true, to_apply=%region_20.25 | all-reduce | flops 64 | bytes 512 | tf_op jit(solution)/shard_map/psum | solution.py:87
  1670.0 234.3 %all-reduce.16.cloned.1.call-done = f32[512,32]{0,1:T(8,128)} async-done(((f32[512,32]{0,1:T(8,128)}), f32[512,32]{0,1:T(8,128)}) %all-reduce.16.cloned.1.call-update) | async-done | bytes 65552 | tf_op jit(solution)/shard_map/psum | solution.py:82
  1910.8 74.4 %psum.91 = f32[32]{0:T(128)S(1)} all-reduce(f32[32]{0:T(128)S(1)} %get-tuple-element.535), channel_id=1, replica_groups=mesh['blk'=64,'col'=4] {'blk','col'}, use_global_device_ids=true, to_apply=%region_30.35 | all-reduce | flops 32 | bytes 256 | tf_op jit(solution)/shard_map/psum | solution.py:87
  1986.0 95.6 %all-gather.9.cloned.1.call-done = f32[8192,32]{0,1:T(8,128)} async-done(((f32[128,32]{0,1:T(8,128)}), f32[8192,32]{0,1:T(8,128)}) %all-gather.9.cloned.1.call-update) | async-done | bytes 1048592 | tf_op jit(solution)/shard_map/all_gather | solution.py:104
  2081.6 3.6 copy.30
  2085.1 144.7 %while.51 = (s32[]{:T(128)}, f32[512,32]{0,1:T(8,128)S(1)}, f32[512]{0:T(512)S(1)}, f32[64,128]{1,0:T(8,128)S(1)}, bf16[64,128,128]{2,1,0:T(8,128)(2,1)}, /*inde...) while((s32[]{:T(128)}, f32[512,32]{0,1:T(8,128)S(1)}, ...), condition=%wide.region_32.37_spmd.clone, body=%wide.region_31.36_spmd.clone.sunk | while | flops 42237952 | bytes 889451 | solution.py:116
  2230.5 21.1 reduce-scatter.6.cloned.1.call-done
  2252.4 77.3 %psum.92 = f32[32]{0:T(128)S(1)} all-reduce(f32[32]{0:T(128)S(1)} %multiply_reduce_fusion.7), channel_id=1, replica_groups=mesh['blk'=64,'col'=4] {'blk','col'}, use_global_device_ids=true, to_apply=%region_35.40 | all-reduce | flops 32 | bytes 256 | tf_op jit(solution)/shard_map/psum | solution.py:121
  2331.6 234.3 %all-reduce.18.cloned.1.call-done = f32[512,32]{0,1:T(8,128)} async-done(((f32[512,32]{0,1:T(8,128)}), f32[512,32]{0,1:T(8,128)}) %all-reduce.18.cloned.1.call-update) | async-done | bytes 65552 | tf_op jit(solution)/shard_map/psum | solution.py:82
  2572.4 74.4 %psum.94 = f32[32]{0:T(128)S(1)} all-reduce(f32[32]{0:T(128)S(1)} %get-tuple-element.537), channel_id=1, replica_groups=mesh['blk'=64,'col'=4] {'blk','col'}, use_global_device_ids=true, to_apply=%region_38.43 | all-reduce | flops 32 | bytes 256 | tf_op jit(solution)/shard_map/psum | solution.py:87
  2647.6 95.6 %all-gather.11.cloned.1.call-done = f32[8192,32]{0,1:T(8,128)} async-done(((f32[128,32]{0,1:T(8,128)}), f32[8192,32]{0,1:T(8,128)}) %all-gather.11.cloned.1.call-update) | async-done | bytes 1048592 | tf_op jit(solution)/shard_map/all_gather | solution.py:104
  2743.2 3.6 copy.31
  2746.7 144.7 %while.52 = (s32[]{:T(128)}, f32[512,32]{0,1:T(8,128)S(1)}, f32[512]{0:T(512)S(1)}, f32[64,128]{1,0:T(8,128)S(1)}, bf16[64,128,128]{2,1,0:T(8,128)(2,1)}, /*inde...) while((s32[]{:T(128)}, f32[512,32]{0,1:T(8,128)S(1)}, ...), condition=%wide.region_40.45_spmd.clone, body=%wide.region_39.44_spmd.clone.sunk | while | flops 42237952 | bytes 889451 | solution.py:116
  2892.1 21.1 reduce-scatter.8.cloned.1.call-done
  2914.8 77.0 %psum.95 = f32[32]{0:T(128)S(1)} all-reduce(f32[32]{0:T(128)S(1)} %multiply_reduce_fusion.5), channel_id=1, replica_groups=mesh['blk'=64,'col'=4] {'blk','col'}, use_global_device_ids=true, to_apply=%region_43.48 | all-reduce | flops 32 | bytes 256 | tf_op jit(solution)/shard_map/psum | solution.py:121
  2991.8 1.4 multiply_subtract_fusion
  (771 shorter events, 469.3 us)
Async XLA Ops:
  7.2 119.0 %copy-start.5 = (bf16[128,128]{1,0:T(8,128)(2,1)S(1)}, bf16[128,128]{1,0:T(8,128)(2,1)}, u32[]{:S(2)}) copy-start(bf16[128,128]{1,0:T(8,128)(2,1)} %param.16) | copy-start | bytes 98308
  7.2 857.6 %all-reduce.10.cloned.1.call-start = ((), (), s32[]{:S(2)}) async-start(), calls=%async_computation.3 | async-start | bytes 2097152 | tf_op jit(solution)/shard_map/psum | solution.py:73
  156.0 708.8 %copy-start.8 = (f32[128,32]{0,1:T(8,128)S(1)}, f32[128,32]{0,1:T(8,128)}, u32[]{:S(2)}) copy-start(f32[128,32]{0,1:T(8,128)} %param.17) | copy-start | bytes 49156
  220.0 736.1 %all-reduce.12.cloned.1.call-start = ((), (), s32[]{:S(2)}) async-start(), calls=%async_computation.4 | async-start | bytes 2097152 | tf_op jit(solution)/shard_map/psum | solution.py:74
  864.8 337.3 %all-reduce.14.cloned.1.call-start = ((), (), s32[]{:S(2)}) async-start(), calls=%async_computation.5 | async-start | bytes 131072 | tf_op jit(solution)/shard_map/psum | solution.py:82
  865.9 449.9 %all-gather.5.cloned.1.call-start = ((), (), s32[]{:S(2)}) async-start(), calls=%async_computation.6 | async-start | bytes 2129920 | tf_op jit(solution)/shard_map/all_gather | solution.py:101
  866.4 554.5 %all-gather.7.cloned.1.call-start = ((), (), s32[]{:S(2)}) async-start(), calls=%async_computation.7 | async-start | bytes 1064960 | tf_op jit(solution)/shard_map/all_gather | solution.py:104
  956.1 1.8 copy-start
  980.2 229.0 %copy-start.6 = (bf16[128,128]{1,0:T(8,128)(2,1)S(1)}, bf16[128,128]{1,0:T(8,128)(2,1)}, u32[]{:S(2)}) copy-start(bf16[128,128]{1,0:T(8,128)(2,1)} %param.16) | copy-start | bytes 98308
  1209.0 381.9 %reduce-scatter.4.cloned.1.call-start = ((), (), s32[]{:S(2)}) async-start(), calls=%async_computation.8 | async-start | bytes 81920 | tf_op jit(solution)/shard_map/reduce_scatter | solution.py:118
  1569.2 0.6 copy-start.1
  1569.9 334.5 %all-reduce.16.cloned.1.call-start = ((), (), s32[]{:S(2)}) async-start(), calls=%async_computation.9 | async-start | bytes 131072 | tf_op jit(solution)/shard_map/psum | solution.py:82
  1670.0 411.6 %all-gather.9.cloned.1.call-start = ((), (), s32[]{:S(2)}) async-start(), calls=%async_computation.10 | async-start | bytes 1064960 | tf_op jit(solution)/shard_map/all_gather | solution.py:104
  1985.9 265.7 %reduce-scatter.6.cloned.1.call-start = ((), (), s32[]{:S(2)}) async-start(), calls=%async_computation.11 | async-start | bytes 81920 | tf_op jit(solution)/shard_map/reduce_scatter | solution.py:118
  1986.0 265.6 %copy-start.4 = (f32[128,32]{0,1:T(8,128)S(1)}, f32[128,32]{0,1:T(8,128)}, u32[]{:S(2)}) copy-start(f32[128,32]{0,1:T(8,128)} %multiply_add_fusion.4) | copy-start | bytes 49156
  2229.8 0.6 copy-start.2
  2230.5 335.5 %all-reduce.18.cloned.1.call-start = ((), (), s32[]{:S(2)}) async-start(), calls=%async_computation.12 | async-start | bytes 131072 | tf_op jit(solution)/shard_map/psum | solution.py:82
  2331.6 411.6 %all-gather.11.cloned.1.call-start = ((), (), s32[]{:S(2)}) async-start(), calls=%async_computation.13 | async-start | bytes 1064960 | tf_op jit(solution)/shard_map/all_gather | solution.py:104
  2647.5 265.7 %reduce-scatter.8.cloned.1.call-start = ((), (), s32[]{:S(2)}) async-start(), calls=%async_computation.14 | async-start | bytes 81920 | tf_op jit(solution)/shard_map/reduce_scatter | solution.py:118
  2647.6 265.6 %copy-start.7 = (f32[128,32]{0,1:T(8,128)S(1)}, f32[128,32]{0,1:T(8,128)}, u32[]{:S(2)}) copy-start(f32[128,32]{0,1:T(8,128)} %multiply_add_fusion.2) | copy-start | bytes 49156
  2891.4 0.6 copy-start.3
Sparse Core Ops, SparseCore 0:
  220.2 644.5 all-reduce.9
  867.6 88.4 all-reduce.11
  962.2 239.8 all-reduce.13
  1205.5 110.2 all-gather.4
  1319.7 101.2 all-gather.6
  1570.0 20.9 reduce-scatter.3
  1670.1 234.2 all-reduce.15
  1986.0 95.4 all-gather.8
  2230.6 20.9 reduce-scatter.5
  2331.7 234.2 all-reduce.17
  2647.6 95.4 all-gather.10
  2892.2 20.9 reduce-scatter.7
